TPU v7x, 256 devices: a whole 4x4x8 slice. The times are simulated.
256 devices in a mesh: gz: 4 (over z_lo, core), xy: 64 (over y, x, z_hi).
Axes of the slice: x: 4, y: 4, z: 8 (z_hi: 4, z_lo: 2; z = z_hi * 2 + z_lo), core: 2. Of those that a mesh axis runs over, the one named last changes fastest.
Arguments:
- features: float32 [64, 128, 28, 256], P('gz', 'xy'), may hold values from -6 to 6
- block_mask: int32 [32, 64, 14], P('gz', 'xy'), may hold values 0 or 1
- near_kernel_weight: float32 [27, 256, 256], P(None, None, 'xy'), may hold values from -0.078125 to 0.078125
- far_kernel_weight: float32 [27, 256, 256], P(None, None, 'xy'), may hold values from -0.078125 to 0.078125
Outputs:
- section_out: float32 [64, 128, 28, 256], P('gz', 'xy')
All inputs are finite; a program needn't handle non-finite values. No bound on the sum of `block_mask` on one device may be relied on, other than what follows from the above.
Results may differ from a plain program's by a relative error of at most 0.00005.
Values sent between devices are 32-bit elements; how exact they have to be, the bound alone decides.
No kernel may reach another device: no remote copies, remote signals or barrier semaphores. Data moves between devices by JAX's collectives and lax.ppermute only.
A program may use at most 128 MiB of HBM per device.

v0:
```python
import jax
import jax.numpy as jnp
from jax import lax
from jax.sharding import PartitionSpec as P

B = 2
NEAR_DILATION = 16
FAR_DILATION = 32


def from_behind(block, axis, distance):
    devices = range(lax.axis_size(axis))
    route = [(i - distance, i) for i in devices if i - distance in devices]
    return lax.ppermute(block, axis, route)


def stack_z(field, step):
    lower = from_behind(field, "gz", step)
    upper = from_behind(field, "gz", -step)
    return jnp.stack((lower, field, upper), 0)


def stack_x(field, step):
    lower = from_behind(field, "xy", step)
    upper = from_behind(field, "xy", -step)
    return jnp.stack((lower, field, upper), 0)


def neighbours(field, step_z, step_x):
    both = stack_x(stack_z(field, step_z), step_x)
    return [[both[col, row] for col in range(3)] for row in range(3)]


def dilated_result(field, weight, dilation):
    slab_z, slab_x, span_y, channels = field.shape
    grid = neighbours(field, dilation // slab_z, dilation // slab_x)
    windows = []
    for row in range(3):
        for col in range(3):
            padded = jnp.pad(grid[row][col], ((0, 0), (0, 0), (dilation, dilation), (0, 0)))
            for lane in range(3):
                windows.append(padded[:, :, lane * dilation : lane * dilation + span_y, :])
    columns = jnp.concatenate(windows, 3).reshape(slab_z * slab_x * span_y, 27 * channels)
    summed = jnp.dot(
        columns,
        weight.reshape(27 * channels, weight.shape[2]),
        precision=lax.Precision.HIGHEST,
        preferred_element_type=jnp.float32,
    )
    return summed.reshape(slab_z, slab_x, span_y, weight.shape[2])


def local(features, block_mask, near_kernel_weight, far_kernel_weight):
    active_blocks = jnp.repeat(jnp.repeat(jnp.repeat(block_mask, B, 0), B, 1), B, 2)
    active_blocks = active_blocks.astype(jnp.float32)[..., None]
    dense_near_output = lax.all_gather(near_kernel_weight, "xy", axis=2, tiled=True)
    masked_input = active_blocks * features
    hidden_state = active_blocks * jnp.maximum(
        dilated_result(masked_input, dense_near_output, NEAR_DILATION), 0.0
    )
    dense_far_output = lax.all_gather(far_kernel_weight, "xy", axis=2, tiled=True)
    return active_blocks * (
        masked_input + dilated_result(hidden_state, dense_far_output, FAR_DILATION)
    )


def solution(mesh):
    in_specs = (
        P("gz", "xy", None, None),
        P("gz", "xy", None),
        P(None, None, "xy"),
        P(None, None, "xy"),
    )
    out_specs = P("gz", "xy", None, None)
    return jax.shard_map(local, mesh=mesh, in_specs=in_specs, out_specs=out_specs, check_vma=False)
```

profile of v0, /device:TPU:10, one launch (start us, length us, event | category | flops | bytes accessed | tf_op | source)
XLA Modules:
  0.0 468.5 jit_solution(18436965677184561776)
XLA Ops:
  6.5 1.6 copy.36
  9.1 1.4 fusion.29
  11.0 1.3 collective-permute-start.1
  12.3 3.1 collective-permute-start
  15.4 1.6 copy.46
  17.0 1.7 copy.70
  20.2 1.6 copy.32
  21.8 4.0 collective-permute-start.2
  25.9 4.2 collective-permute-start.3
  30.5 52.4 %collective-permute-done.2 = f32[3,16,2,28,256]{4,1,3,2,0:T(8,128)S(1)} collective-permute-done((f32[3,16,2,28,256]{4,1,3,2,0:T(8,128)S(1)}, f32[3,16,2,28,256]{4,1,3,2,0:T(8,128)S(1)}, u32[]{:S(2)}, u32[]{:S(2)}) %collective-permute-start.2) | collective-permute-done | bytes 2752544 | tf_op jit(solution)/shard_map/ppermute | solution.py:14
  82.9 1.6 copy.67
  84.5 57.5 %collective-permute-done.3 = f32[3,16,2,28,256]{4,1,3,2,0:T(8,128)S(1)} collective-permute-done((f32[3,16,2,28,256]{4,1,3,2,0:T(8,128)S(1)}, f32[3,16,2,28,256]{4,1,3,2,0:T(8,128)S(1)}, u32[]{:S(2)}, u32[]{:S(2)}) %collective-permute-start.3) | collective-permute-done | bytes 2752544 | tf_op jit(solution)/shard_map/ppermute | solution.py:14
  142.0 1.6 copy.66
  144.0 1.2 fusion.2
  145.2 1.2 constant_dynamic-update-slice_fusion.8
  148.6 1.2 constant_dynamic-update-slice_fusion.7
  151.3 1.2 fusion.6
  152.5 1.2 constant_dynamic-update-slice_fusion.6
  153.6 1.2 fusion.7
  154.8 1.1 fusion.8
  157.0 1.1 fusion.9
  160.4 1.2 fusion.11
  161.6 1.1 fusion.12
  162.8 1.2 constant_dynamic-update-slice_fusion.3
  163.9 1.2 fusion.13
  165.1 1.2 fusion.14
  166.3 1.1 constant_dynamic-update-slice_fusion.2
  167.5 1.2 fusion.15
  168.7 1.1 fusion.16
  169.8 1.1 constant_dynamic-update-slice_fusion.1
  171.0 1.2 fusion.17
  172.2 1.2 fusion.18
  174.5 1.2 fusion.19
  175.7 56.7 %all-gather.3.cloned.1.call-done = f32[27,256,256]{1,0,2:T(8,128)} async-done(((f32[27,256,4]{1,0,2:T(8,128)}), f32[27,256,256]{1,0,2:T(8,128)}) %all-gather.3.cloned.1.call-update) | async-done | bytes 7077904 | tf_op jit(solution)/shard_map/all_gather | solution.py:56
  232.3 10.1 %copy.37 = f32[27,256,256]{2,1,0:T(8,128)} copy(f32[27,256,256]{1,0,2:T(8,128)} %all-gather.3.cloned.1.call-done) | data formatting | bytes 14155776 | tf_op jit(solution)/shard_map/all_gather | solution.py:56
  242.5 27.0 %fusion = f32[16,2,28,256]{3,2,1,0:T(8,128)S(1)} fusion(f32[16,2,28,6912]{3,2,1,0:T(8,128)} %fusion.19, f32[6912,256,1,1]{1,0,3,2:T(8,128)} %bitcast.134, f32[16,28]{1,0:T(8,128)S(1)} %copy.26), kind=kOutput, calls=%fused_computation.25 | convolution fusion | flops 19025821696 | bytes 32769792 | tf_op jit(solution)/shard_map/dot_general | solution.py:44
  270.0 1.3 collective-permute-start.5
  271.3 10.9 %collective-permute-start.4 = (f32[16,2,28,256]{3,0,2,1:T(8,128)S(1)}, f32[16,2,28,256]{3,0,2,1:T(8,128)S(1)}, u32[]{:S(2)}, u32[]{:S(2)}) collective-permute-start(f32[16,2,28,256]{3,0,2,1:T(8,128)S(1)} %copy.38), channel_id=1, source_target_pairs={{0,128},{64,192},{1,129},{65,193},{2,130},{66,194},{3,131},{67,195... | collective-permute-start | bytes 2752520 | tf_op jit(solution)/shard_map/ppermute | solution.py:14
  282.2 31.5 %collective-permute-done.5 = f32[16,2,28,256]{3,0,2,1:T(8,128)S(1)} collective-permute-done((f32[16,2,28,256]{3,0,2,1:T(8,128)S(1)}, f32[16,2,28,256]{3,0,2,1:T(8,128)S(1)}, u32[]{:S(2)}, u32[]{:S(2)}) %collective-permute-start.5) | collective-permute-done | bytes 917536 | tf_op jit(solution)/shard_map/ppermute | solution.py:14
  315.5 3.1 copy.42
  318.6 3.4 collective-permute-start.6
  322.0 3.9 collective-permute-start.7
  326.0 1.1 broadcast_dynamic-update-slice_fusion.16
  327.1 35.3 %all-gather.5.cloned.1.call-done = f32[27,256,256]{1,0,2:T(8,128)} async-done(((f32[27,256,4]{1,0,2:T(8,128)}), f32[27,256,256]{1,0,2:T(8,128)}) %all-gather.5.cloned.1.call-update) | async-done | bytes 7077904 | tf_op jit(solution)/shard_map/all_gather | solution.py:61
  362.4 9.7 %copy.47 = f32[27,256,256]{2,1,0:T(8,128)} copy(f32[27,256,256]{1,0,2:T(8,128)} %all-gather.5.cloned.1.call-done) | data formatting | bytes 14155776 | tf_op jit(solution)/shard_map/all_gather | solution.py:61
  372.1 23.5 %collective-permute-done.6 = f32[3,16,2,28,256]{4,1,3,2,0:T(8,128)} collective-permute-done((f32[3,16,2,28,256]{4,1,3,2,0:T(8,128)}, f32[3,16,2,28,256]{4,1,3,2,0:T(8,128)}, u32[]{:S(2)}, u32[]{:S(2)}) %collective-permute-start.6) | collective-permute-done | bytes 2752544 | tf_op jit(solution)/shard_map/ppermute | solution.py:14
  395.6 3.4 copy.65
  399.0 1.2 fusion.28
  404.7 1.1 broadcast_dynamic-update-slice_fusion.12
  405.8 3.4 copy.64
  409.2 1.2 fusion.26
  410.4 1.2 broadcast_dynamic-update-slice_fusion.11
  413.8 1.1 broadcast_dynamic-update-slice_fusion.9
  417.1 1.2 broadcast_dynamic-update-slice_fusion.7
  419.4 1.2 fusion.23
  420.6 1.2 broadcast_dynamic-update-slice_fusion.5
  421.8 1.2 broadcast_dynamic-update-slice_fusion.4
  423.0 1.1 fusion.22
  424.1 1.2 broadcast_dynamic-update-slice_fusion.3
  427.6 1.2 broadcast_dynamic-update-slice_fusion.1
  428.8 1.2 broadcast_dynamic-update-slice_fusion
  431.0 1.2 broadcast_dynamic-update-slice_fusion.17
  432.3 27.5 %fusion.1 = f32[16,2,28,256]{3,2,1,0:T(8,128)S(1)} fusion(f32[16,2,28,6912]{3,2,1,0:T(8,128)} %broadcast_dynamic-update-slice_fusion.17, f32[6912,256,1,1]{1,0,3,2:T(8,128)S(1)} %bitcast.125, f32[16,28]{1,0:T(8,128)S(1)} %copy.26, f32[16,2,28,256]{3,1,2,0:T(2,128)S(1)} %copy-done), kind=kOutput, calls=%fused_computation.27 | convolution fusion | flops 19026051072 | bytes 33687296 | tf_op jit(solution)/shard_map/dot_general | solution.py:44
  459.8 1.6 copy.48
  (50 shorter events, 27.7 us)
Async XLA Ops:
  6.5 225.8 %all-gather.3.cloned.1.call-start = ((), (), s32[]{:S(2)}) async-start(), calls=%async_computation | async-start | bytes 8519680 | tf_op jit(solution)/shard_map/all_gather | solution.py:56
  8.1 354.3 %all-gather.5.cloned.1.call-start = ((), (), s32[]{:S(2)}) async-start(), calls=%async_computation.1 | async-start | bytes 8519680 | tf_op jit(solution)/shard_map/all_gather | solution.py:61
  11.0 6.0 %collective-permute-start.1 = (f32[16,2,28,256]{3,0,2,1:T(8,128)S(1)}, f32[16,2,28,256]{3,0,2,1:T(8,128)}, u32[]{:S(2)}, u32[]{:S(2)}) collective-permute-start(f32[16,2,28,256]{3,0,2,1:T(8,128)S(1)} %copy.28), channel_id=1, source_target_pairs={{64,0},{128,64},{192,128},{65,1},{129,65},{193,129},{66,2},{130,66... | collective-permute-start | bytes 2752520 | tf_op jit(solution)/shard_map/ppermute | solution.py:14
  12.3 6.4 %collective-permute-start = (f32[16,2,28,256]{3,0,2,1:T(8,128)S(1)}, f32[16,2,28,256]{3,0,2,1:T(8,128)S(1)}, u32[]{:S(2)}, u32[]{:S(2)}) collective-permute-start(f32[16,2,28,256]{3,0,2,1:T(8,128)S(1)} %copy.28), channel_id=1, source_target_pairs={{0,64},{64,128},{128,192},{1,65},{65,129},{129,193},{2,66},{66,130... | collective-permute-start | bytes 2752520 | tf_op jit(solution)/shard_map/ppermute | solution.py:14
  21.8 61.1 %collective-permute-start.2 = (f32[3,16,2,28,256]{4,1,3,2,0:T(8,128)S(1)}, f32[3,16,2,28,256]{4,1,3,2,0:T(8,128)S(1)}, u32[]{:S(2)}, u32[]{:S(2)}) collective-permute-start(f32[3,16,2,28,256]{4,1,3,2,0:T(8,128)S(1)} %copy.32), channel_id=1, source_target_pairs={{0,8},{1,9},{2,10},{3,11},{4,12},{5,13},{6,14},{7,15},{8,16},{9,17... | collective-permute-start | bytes 8257544 | tf_op jit(solution)/shard_map/ppermute | solution.py:14
  25.9 116.1 %collective-permute-start.3 = (f32[3,16,2,28,256]{4,1,3,2,0:T(8,128)S(1)}, f32[3,16,2,28,256]{4,1,3,2,0:T(8,128)S(1)}, u32[]{:S(2)}, u32[]{:S(2)}) collective-permute-start(f32[3,16,2,28,256]{4,1,3,2,0:T(8,128)S(1)} %copy.32), channel_id=1, source_target_pairs={{8,0},{9,1},{10,2},{11,3},{12,4},{13,5},{14,6},{15,7},{16,8},{17,9... | collective-permute-start | bytes 8257544 | tf_op jit(solution)/shard_map/ppermute | solution.py:14
  270.0 43.7 %collective-permute-start.5 = (f32[16,2,28,256]{3,0,2,1:T(8,128)S(1)}, f32[16,2,28,256]{3,0,2,1:T(8,128)S(1)}, u32[]{:S(2)}, u32[]{:S(2)}) collective-permute-start(f32[16,2,28,256]{3,0,2,1:T(8,128)S(1)} %copy.38), channel_id=1, source_target_pairs={{128,0},{192,64},{129,1},{193,65},{130,2},{194,66},{131,3},{195,67... | collective-permute-start | bytes 2752520 | tf_op jit(solution)/shard_map/ppermute | solution.py:14
  271.3 42.9 %collective-permute-start.4 = (f32[16,2,28,256]{3,0,2,1:T(8,128)S(1)}, f32[16,2,28,256]{3,0,2,1:T(8,128)S(1)}, u32[]{:S(2)}, u32[]{:S(2)}) collective-permute-start(f32[16,2,28,256]{3,0,2,1:T(8,128)S(1)} %copy.38), channel_id=1, source_target_pairs={{0,128},{64,192},{1,129},{65,193},{2,130},{66,194},{3,131},{67,195... | collective-permute-start | bytes 2752520 | tf_op jit(solution)/shard_map/ppermute | solution.py:14
  318.6 76.9 %collective-permute-start.6 = (f32[3,16,2,28,256]{4,1,3,2,0:T(8,128)}, f32[3,16,2,28,256]{4,1,3,2,0:T(8,128)}, u32[]{:S(2)}, u32[]{:S(2)}) collective-permute-start(f32[3,16,2,28,256]{4,1,3,2,0:T(8,128)} %copy.42), channel_id=1, source_target_pairs={{0,16},{1,17},{2,18},{3,19},{4,20},{5,21},{6,22},{7,23},{8,24},{9,... | collective-permute-start | bytes 8257544 | tf_op jit(solution)/shard_map/ppermute | solution.py:14
  322.0 83.8 %collective-permute-start.7 = (f32[3,16,2,28,256]{4,1,3,2,0:T(8,128)}, f32[3,16,2,28,256]{4,1,3,2,0:T(8,128)}, u32[]{:S(2)}, u32[]{:S(2)}) collective-permute-start(f32[3,16,2,28,256]{4,1,3,2,0:T(8,128)} %copy.42), channel_id=1, source_target_pairs={{16,0},{17,1},{18,2},{19,3},{20,4},{21,5},{22,6},{23,7},{24,8},{25... | collective-permute-start | bytes 8257544 | tf_op jit(solution)/shard_map/ppermute | solution.py:14
  372.1 60.1 %slice-start = ((s8[7077888]{0:T(1024)(128)(4,1)}), s8[4194304]{0:T(1024)(128)(4,1)S(1)}, s32[]{:S(2)}) async-start(s8[7077888]{0:T(1024)(128)(4,1)} %bitcast.123), calls=%async_computation.2 | async-start | bytes 8388608
  372.1 60.1 %copy-start = (f32[16,2,28,256]{3,1,2,0:T(2,128)S(1)}, f32[16,2,28,256]{3,1,2,0:T(2,128)}, u32[]{:S(2)}) copy-start(f32[16,2,28,256]{3,1,2,0:T(2,128)} %param.4) | copy-start | bytes 2752516
  411.5 20.7 %slice-start.1 = ((s8[7077888]{0:T(1024)(128)(4,1)}), s8[2883584]{0:T(1024)(128)(4,1)S(1)}, s32[]{:S(2)}) async-start(s8[7077888]{0:T(1024)(128)(4,1)} %bitcast.123), calls=%async_computation.3 | async-start | bytes 5767168
Sparse Core Ops, SparseCore 0:
  10.6 221.6 all-gather.2
  235.6 126.7 all-gather.4
where the time goes:
time: 478 us; the launch traced here: 468 us
  waiting for transfers between devices  257 us (54%)
  local copies, waits for them, and re-layouts  107 us (22%)
  matrix products  54.5 us (11%)
  starting transfers between devices  32.2 us (7%)
  between operations  13.9 us (3%)
    ppermute x8, waiting for transfers between devices, from_behind(): return lax.ppermute(block, axis, route)  165 us
    unnamed x60, local copies, waits for them, and re-layouts  63 us
    all_gather x1, waiting for transfers between devices, local(): lax.all_gather(near_kernel_weight, 'xy', axis=2, tiled=True)  56.7 us
    dot_general x2, matrix products, dilated_result(): jnp.dot(columns, weight.reshape(27 * channels, weight.shape[2]), precisio...  54.5 us
    all_gather x1, waiting for transfers between devices, local(): lax.all_gather(far_kernel_weight, 'xy', axis=2, tiled=True)  35.3 us
    ppermute x8, starting transfers between devices, from_behind(): return lax.ppermute(block, axis, route)  32.1 us
    ppermute x8, local copies, waits for them, and re-layouts, from_behind(): return lax.ppermute(block, axis, route)  13.3 us
    all_gather x1, local copies, waits for them, and re-layouts, local(): lax.all_gather(near_kernel_weight, 'xy', axis=2, tiled=True)  10.1 us
  transfers between devices with their start and end apart: 10, of which 6 were waited for; matrix products, arithmetic and copies ran while one was open for 23% of the time, Pallas kernels for 0%

commit v1 on v0

--- a/solution.py
+++ b/solution.py
@@ -53,7 +53,9 @@
 def local(features, block_mask, near_kernel_weight, far_kernel_weight):
     active_blocks = jnp.repeat(jnp.repeat(jnp.repeat(block_mask, B, 0), B, 1), B, 2)
     active_blocks = active_blocks.astype(jnp.float32)[..., None]
-    dense_near_output = lax.all_gather(near_kernel_weight, "xy", axis=2, tiled=True)
+    dense_near_output = jnp.concatenate(
+        lax.all_to_all(jnp.stack([near_kernel_weight] * lax.axis_size("xy")), "xy", 0, 0), axis=2
+    )
     masked_input = active_blocks * features
     hidden_state = active_blocks * jnp.maximum(
         dilated_result(masked_input, dense_near_output, NEAR_DILATION), 0.0

time: 478 us -> 541 us (1.13)
  starting transfers between devices: 32.2 us -> 170 us
  waiting for transfers between devices: 257 us -> 179 us
    ppermute x8, starting transfers between devices: 32.1 us -> 155 us  [from_behind(): return lax.ppermute(block, axis, route)]
    all_gather x1 -> x0, waiting for transfers between devices: 56.7 us -> none  [local(): lax.all_gather(near_kernel_weight, 'xy', axis=2, tiled=True)]
    all_gather x1, waiting for transfers between devices: 35.3 us -> 0.01 us  [local(): lax.all_gather(far_kernel_weight, 'xy', axis=2, tiled=True)]
    all_to_all x0 -> x1, starting transfers between devices: none -> 14.7 us  [local(): lax.all_to_all(jnp.stack([near_kernel_weight] * lax.axis_size('xy')), 'xy...]
    ppermute x8, waiting for transfers between devices: 165 us -> 179 us  [from_behind(): return lax.ppermute(block, axis, route)]
    all_gather x1 -> x0, local copies, waits for them, and re-layouts: 10.1 us -> none  [local(): lax.all_gather(near_kernel_weight, 'xy', axis=2, tiled=True)]
  transfers between devices with their start and end apart: 10 -> 10, of which waited for: 6 -> 5; matrix products, arithmetic and copies ran while one was open for 23% -> 21% of each run, Pallas kernels for 0% -> 0%
where the time goes in v1:
time: 541 us; the launch traced here: 533 us
  waiting for transfers between devices  179 us (33%)
  starting transfers between devices  170 us (31%)
  local copies, waits for them, and re-layouts  112 us (21%)
  matrix products  54.6 us (10%)
  between operations  13.8 us (3%)
    ppermute x8, waiting for transfers between devices, from_behind(): return lax.ppermute(block, axis, route)  179 us
    ppermute x8, starting transfers between devices, from_behind(): return lax.ppermute(block, axis, route)  155 us
    unnamed x60, local copies, waits for them, and re-layouts  68.3 us
    dot_general x2, matrix products, dilated_result(): jnp.dot(columns, weight.reshape(27 * channels, weight.shape[2]), precisio...  54.6 us
    all_to_all x1, starting transfers between devices, local(): lax.all_to_all(jnp.stack([near_kernel_weight] * lax.axis_size('xy')), 'xy...  14.7 us
    ppermute x8, local copies, waits for them, and re-layouts, from_behind(): return lax.ppermute(block, axis, route)  13.3 us
  transfers between devices with their start and end apart: 10, of which 5 were waited for; matrix products, arithmetic and copies ran while one was open for 21% of the time, Pallas kernels for 0%

profile of v1, /device:TPU:10, one launch (start us, length us, event | category | flops | bytes accessed | tf_op | source)
XLA Modules:
  0.0 532.5 jit_solution(3817843006018019465)
XLA Ops:
  6.5 4.7 stack.37
  11.2 14.7 %all-to-all-start = ((f32[64,27,256,4]{2,3,1,0:T(4,128)}), f32[64,27,256,4]{2,3,1,0:T(4,128)}, u32[]{:S(2)}, u32[]{:S(2)}) async-start(f32[64,27,256,4]{2,3,1,0:T(4,128)} %stack.37), calls=%async_computation | async-start | bytes 14155776 | tf_op jit(solution)/shard_map/all_to_all | solution.py:57
  26.9 1.4 fusion.36
  28.8 1.3 collective-permute-start.1
  30.1 3.1 collective-permute-start
  33.2 1.6 copy.48
  34.9 1.7 copy.74
  38.1 1.6 copy.34
  39.6 4.0 collective-permute-start.2
  43.7 4.4 collective-permute-start.3
  48.5 62.1 %collective-permute-done.2 = f32[3,16,2,28,256]{4,1,3,2,0:T(8,128)S(1)} collective-permute-done((f32[3,16,2,28,256]{4,1,3,2,0:T(8,128)S(1)}, f32[3,16,2,28,256]{4,1,3,2,0:T(8,128)S(1)}, u32[]{:S(2)}, u32[]{:S(2)}) %collective-permute-start.2) | collective-permute-done | bytes 2752544 | tf_op jit(solution)/shard_map/ppermute | solution.py:14
  110.5 1.6 copy.71
  112.1 52.0 %collective-permute-done.3 = f32[3,16,2,28,256]{4,1,3,2,0:T(8,128)S(1)} collective-permute-done((f32[3,16,2,28,256]{4,1,3,2,0:T(8,128)S(1)}, f32[3,16,2,28,256]{4,1,3,2,0:T(8,128)S(1)}, u32[]{:S(2)}, u32[]{:S(2)}) %collective-permute-start.3) | collective-permute-done | bytes 2752544 | tf_op jit(solution)/shard_map/ppermute | solution.py:14
  164.2 1.6 copy.70
  167.3 1.2 constant_dynamic-update-slice_fusion.8
  168.5 1.1 fusion.10
  169.6 1.2 fusion.11
  173.5 1.2 fusion.13
  175.8 1.2 fusion.14
  176.9 1.2 fusion.15
  178.1 1.2 constant_dynamic-update-slice_fusion.5
  180.4 1.1 fusion.17
  183.8 1.1 fusion.19
  184.9 1.2 constant_dynamic-update-slice_fusion.3
  187.2 1.2 fusion.21
  188.4 1.2 constant_dynamic-update-slice_fusion.2
  189.6 1.2 fusion.22
  190.8 1.2 fusion.23
  192.0 1.2 constant_dynamic-update-slice_fusion.1
  193.1 1.1 fusion.24
  194.3 1.2 fusion.25
  195.5 1.2 constant_dynamic-update-slice_fusion
  196.7 1.2 fusion.26
  197.8 4.7 copy.38
  202.6 6.7 %copy.54 = f32[32,8,27,256]{3,1,2,0:T(8,128)S(1)} copy(f32[32,8,27,256]{3,2,1,0:T(8,128)S(1)} %bitcast.130) | data formatting | bytes 14155776
  209.3 27.1 %fusion.5 = f32[16,2,28,256]{3,2,1,0:T(8,128)S(1)} fusion(f32[16,2,28,6912]{3,2,1,0:T(8,128)} %fusion.26, f32[6912,256]{0,1:T(8,128)S(1)} %bitcast.142, f32[16,28]{1,0:T(8,128)S(1)} %copy.28), kind=kOutput, calls=%fused_computation.27 | convolution fusion | flops 19025821696 | bytes 32769792 | tf_op jit(solution)/shard_map/dot_general | solution.py:44
  237.0 1.3 collective-permute-start.5
  238.3 133.5 %collective-permute-start.4 = (f32[16,2,28,256]{3,0,2,1:T(8,128)S(1)}, f32[16,2,28,256]{3,0,2,1:T(8,128)S(1)}, u32[]{:S(2)}, u32[]{:S(2)}) collective-permute-start(f32[16,2,28,256]{3,0,2,1:T(8,128)S(1)} %copy.40), channel_id=1, source_target_pairs={{0,128},{64,192},{1,129},{65,193},{2,130},{66,194},{3,131},{67,195... | collective-permute-start | bytes 2752520 | tf_op jit(solution)/shard_map/ppermute | solution.py:14
  371.7 18.7 %collective-permute-done.5 = f32[16,2,28,256]{3,0,2,1:T(8,128)S(1)} collective-permute-done((f32[16,2,28,256]{3,0,2,1:T(8,128)S(1)}, f32[16,2,28,256]{3,0,2,1:T(8,128)S(1)}, u32[]{:S(2)}, u32[]{:S(2)}) %collective-permute-start.5) | collective-permute-done | bytes 917536 | tf_op jit(solution)/shard_map/ppermute | solution.py:14
  392.9 3.1 copy.44
  396.1 3.4 collective-permute-start.6
  399.5 3.9 collective-permute-start.7
  404.5 9.7 %copy.49 = f32[27,256,256]{2,1,0:T(8,128)} copy(f32[27,256,256]{1,0,2:T(8,128)} %all-gather.2.cloned.1.call-done) | data formatting | bytes 14155776 | tf_op jit(solution)/shard_map/all_gather | solution.py:63
  414.2 45.4 %collective-permute-done.6 = f32[3,16,2,28,256]{4,1,3,2,0:T(8,128)} collective-permute-done((f32[3,16,2,28,256]{4,1,3,2,0:T(8,128)}, f32[3,16,2,28,256]{4,1,3,2,0:T(8,128)}, u32[]{:S(2)}, u32[]{:S(2)}) %collective-permute-start.6) | collective-permute-done | bytes 2752544 | tf_op jit(solution)/shard_map/ppermute | solution.py:14
  459.6 3.4 copy.69
  463.0 1.2 fusion.35
  464.2 1.1 broadcast_dynamic-update-slice_fusion.15
  465.4 1.2 broadcast_dynamic-update-slice_fusion.14
  468.8 1.2 broadcast_dynamic-update-slice_fusion.12
  469.9 3.4 copy.68
  474.5 1.1 broadcast_dynamic-update-slice_fusion.11
  475.6 1.2 broadcast_dynamic-update-slice_fusion.10
  476.8 1.2 fusion.32
  483.5 1.2 fusion.30
  485.8 1.2 broadcast_dynamic-update-slice_fusion.4
  487.0 1.2 fusion.29
  488.2 1.2 broadcast_dynamic-update-slice_fusion.3
  489.4 1.1 broadcast_dynamic-update-slice_fusion.2
  490.5 1.1 fusion.28
  492.8 1.2 broadcast_dynamic-update-slice_fusion
  493.9 1.2 fusion.27
  495.2 1.2 broadcast_dynamic-update-slice_fusion.17
  496.3 27.5 %fusion.8 = f32[16,2,28,256]{3,2,1,0:T(8,128)S(1)} fusion(f32[16,2,28,6912]{3,2,1,0:T(8,128)} %broadcast_dynamic-update-slice_fusion.17, f32[6912,256,1,1]{1,0,3,2:T(8,128)S(1)} %bitcast.133, f32[16,28]{1,0:T(8,128)S(1)} %copy.28, f32[16,2,28,256]{3,1,2,0:T(2,128)S(1)} %copy-done), kind=kOutput, calls=%fused_computation.29 | convolution fusion | flops 19026051072 | bytes 33687296 | tf_op jit(solution)/shard_map/dot_general | solution.py:44
  523.9 1.6 copy.50
  (50 shorter events, 28.4 us)
Async XLA Ops:
  11.2 186.6 %all-to-all-start = ((f32[64,27,256,4]{2,3,1,0:T(4,128)}), f32[64,27,256,4]{2,3,1,0:T(4,128)}, u32[]{:S(2)}, u32[]{:S(2)}) async-start(f32[64,27,256,4]{2,3,1,0:T(4,128)} %stack.37), calls=%async_computation | async-start | bytes 14155776 | tf_op jit(solution)/shard_map/all_to_all | solution.py:57
  25.9 378.6 %all-gather.2.cloned.1.call-start = ((), (), s32[]{:S(2)}) async-start(), calls=%async_computation.1 | async-start | bytes 8519680 | tf_op jit(solution)/shard_map/all_gather | solution.py:63
  28.8 6.0 %collective-permute-start.1 = (f32[16,2,28,256]{3,0,2,1:T(8,128)S(1)}, f32[16,2,28,256]{3,0,2,1:T(8,128)}, u32[]{:S(2)}, u32[]{:S(2)}) collective-permute-start(f32[16,2,28,256]{3,0,2,1:T(8,128)S(1)} %copy.30), channel_id=1, source_target_pairs={{64,0},{128,64},{192,128},{65,1},{129,65},{193,129},{66,2},{130,66... | collective-permute-start | bytes 2752520 | tf_op jit(solution)/shard_map/ppermute | solution.py:14
  30.1 6.4 %collective-permute-start = (f32[16,2,28,256]{3,0,2,1:T(8,128)S(1)}, f32[16,2,28,256]{3,0,2,1:T(8,128)S(1)}, u32[]{:S(2)}, u32[]{:S(2)}) collective-permute-start(f32[16,2,28,256]{3,0,2,1:T(8,128)S(1)} %copy.30), channel_id=1, source_target_pairs={{0,64},{64,128},{128,192},{1,65},{65,129},{129,193},{2,66},{66,130... | collective-permute-start | bytes 2752520 | tf_op jit(solution)/shard_map/ppermute | solution.py:14
  39.6 70.9 %collective-permute-start.2 = (f32[3,16,2,28,256]{4,1,3,2,0:T(8,128)S(1)}, f32[3,16,2,28,256]{4,1,3,2,0:T(8,128)S(1)}, u32[]{:S(2)}, u32[]{:S(2)}) collective-permute-start(f32[3,16,2,28,256]{4,1,3,2,0:T(8,128)S(1)} %copy.34), channel_id=1, source_target_pairs={{0,8},{1,9},{2,10},{3,11},{4,12},{5,13},{6,14},{7,15},{8,16},{9,17... | collective-permute-start | bytes 8257544 | tf_op jit(solution)/shard_map/ppermute | solution.py:14
  43.7 120.5 %collective-permute-start.3 = (f32[3,16,2,28,256]{4,1,3,2,0:T(8,128)S(1)}, f32[3,16,2,28,256]{4,1,3,2,0:T(8,128)S(1)}, u32[]{:S(2)}, u32[]{:S(2)}) collective-permute-start(f32[3,16,2,28,256]{4,1,3,2,0:T(8,128)S(1)} %copy.34), channel_id=1, source_target_pairs={{8,0},{9,1},{10,2},{11,3},{12,4},{13,5},{14,6},{15,7},{16,8},{17,9... | collective-permute-start | bytes 8257544 | tf_op jit(solution)/shard_map/ppermute | solution.py:14
  237.0 153.5 %collective-permute-start.5 = (f32[16,2,28,256]{3,0,2,1:T(8,128)S(1)}, f32[16,2,28,256]{3,0,2,1:T(8,128)S(1)}, u32[]{:S(2)}, u32[]{:S(2)}) collective-permute-start(f32[16,2,28,256]{3,0,2,1:T(8,128)S(1)} %copy.40), channel_id=1, source_target_pairs={{128,0},{192,64},{129,1},{193,65},{130,2},{194,66},{131,3},{195,67... | collective-permute-start | bytes 2752520 | tf_op jit(solution)/shard_map/ppermute | solution.py:14
  238.3 153.4 %collective-permute-start.4 = (f32[16,2,28,256]{3,0,2,1:T(8,128)S(1)}, f32[16,2,28,256]{3,0,2,1:T(8,128)S(1)}, u32[]{:S(2)}, u32[]{:S(2)}) collective-permute-start(f32[16,2,28,256]{3,0,2,1:T(8,128)S(1)} %copy.40), channel_id=1, source_target_pairs={{0,128},{64,192},{1,129},{65,193},{2,130},{66,194},{3,131},{67,195... | collective-permute-start | bytes 2752520 | tf_op jit(solution)/shard_map/ppermute | solution.py:14
  396.1 63.5 %collective-permute-start.6 = (f32[3,16,2,28,256]{4,1,3,2,0:T(8,128)}, f32[3,16,2,28,256]{4,1,3,2,0:T(8,128)}, u32[]{:S(2)}, u32[]{:S(2)}) collective-permute-start(f32[3,16,2,28,256]{4,1,3,2,0:T(8,128)} %copy.44), channel_id=1, source_target_pairs={{0,16},{1,17},{2,18},{3,19},{4,20},{5,21},{6,22},{7,23},{8,24},{9,... | collective-permute-start | bytes 8257544 | tf_op jit(solution)/shard_map/ppermute | solution.py:14
  399.5 70.5 %collective-permute-start.7 = (f32[3,16,2,28,256]{4,1,3,2,0:T(8,128)}, f32[3,16,2,28,256]{4,1,3,2,0:T(8,128)}, u32[]{:S(2)}, u32[]{:S(2)}) collective-permute-start(f32[3,16,2,28,256]{4,1,3,2,0:T(8,128)} %copy.44), channel_id=1, source_target_pairs={{16,0},{17,1},{18,2},{19,3},{20,4},{21,5},{22,6},{23,7},{24,8},{25... | collective-permute-start | bytes 8257544 | tf_op jit(solution)/shard_map/ppermute | solution.py:14
  414.2 82.1 %slice-start = ((s8[7077888]{0:T(1024)(128)(4,1)}), s8[4194304]{0:T(1024)(128)(4,1)S(1)}, s32[]{:S(2)}) async-start(s8[7077888]{0:T(1024)(128)(4,1)} %bitcast.131), calls=%async_computation.2 | async-start | bytes 8388608
  414.2 82.1 %copy-start = (f32[16,2,28,256]{3,1,2,0:T(2,128)S(1)}, f32[16,2,28,256]{3,1,2,0:T(2,128)}, u32[]{:S(2)}) copy-start(f32[16,2,28,256]{3,1,2,0:T(2,128)} %param.4) | copy-start | bytes 2752516
  475.6 20.7 %slice-start.1 = ((s8[7077888]{0:T(1024)(128)(4,1)}), s8[2883584]{0:T(1024)(128)(4,1)S(1)}, s32[]{:S(2)}) async-start(s8[7077888]{0:T(1024)(128)(4,1)} %bitcast.131), calls=%async_computation.3 | async-start | bytes 5767168
Sparse Core Ops, SparseCore 0:
  35.0 218.0 all-gather.1
